TPU v7x, 512 devices: a whole 4x8x8 slice. The times are simulated.
512 devices in a mesh: row: 32 (over z_hi, y, core), col: 16 (over z_lo, x).
Axes of the slice: x: 4, y: 8, z: 8 (z_hi: 2, z_lo: 4; z = z_hi * 4 + z_lo), core: 2. Of those that a mesh axis runs over, the one named last changes fastest.
Arguments:
- mask_logits: float32 [4096, 2048], P('row', 'col'), may hold values from -6 to 6
- target: float32 [4096, 2048], P('row', 'col'), may hold values from 0 to 1
- weight: float32 [4096, 2048], P('row', 'col'), may hold values from 0.004 to 10, as said below
- kernels: float32 [2, 12288], P(None, ('row', 'col')), may hold values from -3 to 3
Outputs:
- new_logits: float32 [4096, 2048], P('row', 'col')
- loss_value: float32 [], replicated
Inputs may be any that keep to these rules, and one draw needn't show every extreme that they name: `weight`: positive loss weights.
All inputs are finite; a program needn't handle non-finite values.
Results may differ from a plain program's by a relative error of at most 0.0003.
Values sent between devices are 32-bit elements; how exact they have to be, the bound alone decides.
A program may use at most 64 MiB of HBM per device.

v0:
```python
import math

import jax
import jax.numpy as jnp
from jax import lax
from jax.sharding import PartitionSpec as P

HALO = 64
KERNELS = 6
BAND = 32
CONDITIONS = 2


SHARPNESS = 6.0
THRESHOLD = 0.75
STEP = 0.5
EPSILON = 1e-06
DOSES = (1.0, 1.15)


def padded_2(block, sides, width):
    for axis, dim in sides:
        count = lax.axis_size(axis)
        forward = [(i, i + 1) for i in range(count - 1)]
        backward = [(target, source) for source, target in forward]
        low = lax.ppermute(
            lax.slice_in_dim(block, block.shape[dim] - width, None, axis=dim), axis, forward
        )
        high = lax.ppermute(lax.slice_in_dim(block, 0, width, axis=dim), axis, backward)
        block = jnp.concatenate([low, block, high], axis=dim)
    return block


def matmul(first, second):
    return jnp.matmul(
        first, second, precision=lax.Precision.HIGHEST, preferred_element_type=jnp.float32
    )


def cmatmul(first_re, first_im, second_re, second_im):
    return (
        matmul(first_re, second_re) - matmul(first_im, second_im),
        matmul(first_re, second_im) + matmul(first_im, second_re),
    )


def dft_rows(band, pad_width):
    freq = jnp.arange(band, dtype=jnp.int32) - band // 2
    place = jnp.arange(pad_width, dtype=jnp.int32)
    turns = (freq[:, None] * place[None, :] % pad_width).astype(jnp.float32) * (
        2.0 * math.pi / pad_width
    )
    factor = 1.0 / math.sqrt(pad_width)
    return (jnp.cos(turns) * factor, -jnp.sin(turns) * factor)


def synthesize(spec_re, spec_im, wave_re, wave_im):
    left_re, left_im = cmatmul(wave_re.T, -wave_im.T, spec_re, spec_im)
    return cmatmul(left_re, left_im, wave_re, -wave_im)


def analyse(cell_re, cell_im, wave_re, wave_im):
    left_re, left_im = cmatmul(wave_re, wave_im, cell_re, cell_im)
    return cmatmul(left_re, left_im, wave_re.T, wave_im.T)


def tile_terms(padded_tile, kernel_re, kernel_im, wave_re, wave_im, dose, margin):
    mask_tile, target_tile, weight_tile = (padded_tile[0], padded_tile[1], padded_tile[2])
    pad_width = mask_tile.shape[0]
    core_width = pad_width - 2 * margin
    four_re, four_im = cmatmul(
        matmul(wave_re, mask_tile), matmul(wave_im, mask_tile), wave_re.T, wave_im.T
    )
    prod_re = four_re[None] * kernel_re - four_im[None] * kernel_im
    prod_im = four_re[None] * kernel_im + four_im[None] * kernel_re
    fields_re, fields_im = synthesize(prod_re, prod_im, wave_re, wave_im)
    intensity = jnp.sum(fields_re * fields_re + fields_im * fields_im, axis=0)
    resist = jax.nn.sigmoid(SHARPNESS * (dose * intensity - THRESHOLD))
    error_map = resist - target_tile
    inner = (weight_tile * error_map * error_map)[
        margin : margin + core_width, margin : margin + core_width
    ]
    tile_loss = jnp.sum(inner)
    slope_map = 2.0 * SHARPNESS * dose * weight_tile * error_map * resist * (1.0 - resist)
    back_re, back_im = analyse(
        slope_map[None] * fields_re, slope_map[None] * fields_im, wave_re, wave_im
    )
    sum_re = jnp.sum(kernel_re * back_re + kernel_im * back_im, axis=0)
    sum_im = jnp.sum(kernel_re * back_im - kernel_im * back_re, axis=0)
    core_re = wave_re[:, margin : margin + core_width]
    core_im = wave_im[:, margin : margin + core_width]
    left_re, left_im = cmatmul(core_re.T, -core_im.T, sum_re, sum_im)
    real_part = matmul(left_re, core_re) + matmul(left_im, core_im)
    return (2.0 * real_part, tile_loss)


def shards(mask_logits, target, weight, kernels):
    mask_cells = jax.nn.sigmoid(mask_logits)
    stacked = jnp.stack([mask_cells, target, weight])
    padded = padded_2(stacked, (("row", 1), ("col", 2)), HALO)
    core_width = mask_logits.shape[0]
    tile_count = mask_logits.shape[1] // core_width
    pad_width = core_width + 2 * HALO
    wave_re, wave_im = dft_rows(BAND, pad_width)
    whole_bank = lax.all_gather(kernels, ("row", "col"), axis=1, tiled=True)
    tile_grads = [jnp.zeros((core_width, core_width), jnp.float32)]
    loss_global = jnp.float32(0.0)
    for condition in range(CONDITIONS):
        flat_bank = whole_bank[condition]
        spectra = flat_bank.reshape(2, KERNELS, BAND, BAND)
        condition_loss = jnp.float32(0.0)
        part_grad, part_loss = tile_terms(
            padded, spectra[0], spectra[1], wave_re, wave_im, DOSES[condition], HALO
        )
        tile_grads[0] = tile_grads[0] + part_grad
        condition_loss = part_loss
        loss_global = loss_global + lax.psum(condition_loss, ("row", "col"))
    grad_cells = tile_grads[0] * mask_cells * (1.0 - mask_cells)
    square_local = jnp.sum(grad_cells * grad_cells)
    square_global = lax.psum(square_local, ("row", "col"))
    cell_count = lax.axis_size("row") * core_width * lax.axis_size("col") * core_width * tile_count
    loss_value = loss_global / cell_count
    norm_value = jnp.sqrt(square_global / cell_count + EPSILON)
    return (mask_logits - STEP * grad_cells / norm_value, loss_value)


def solution(mesh):
    placed = (P("row", "col"), P("row", "col"), P("row", "col"), P(None, ("row", "col")))
    return jax.shard_map(
        shards, mesh=mesh, in_specs=placed, out_specs=(P("row", "col"), P()), check_vma=False
    )
```

profile of v0, /device:TPU:1, one launch (start us, length us, event | category | flops | bytes accessed | tf_op | source)
XLA Modules:
  0.0 1497.9 jit_solution(4228233007003579788)
XLA Ops:
  0.6 0.9 fusion.144
  1.5 0.9 pad_maximum_fusion.2
  2.4 8.9 collective-permute-start.1
  11.3 1.9 collective-permute-start
  13.3 1216.6 %all-gather = f32[512,24,2]{1,2,0:T(2,128)S(1)} all-gather(f32[1,24,2]{1,2,0:T(2,128)} %bitcast.232), channel_id=1, replica_groups=mesh['row'=32,'col'=16] {'row','col'}, dimensions={0}, use_global_device_ids=true | all-gather | bytes 98496 | tf_op jit(solution)/shard_map/all_gather | solution.py:105
  1231.1 1.3 collective-permute-start.3
  1232.4 4.2 collective-permute-start.2
  1236.6 0.8 negate_multiply_fusion
  1237.4 2.5 collective-permute-done.3
  1239.9 1.2 collective-permute-done.2
  1244.2 0.7 multiply_add_fusion
  1245.6 0.5 fusion.140
  1246.2 0.5 fusion.141
  1246.7 0.5 fusion.134
  1247.2 1.6 fusion.70
  1248.8 2.5 fusion.68
  1251.3 1.6 copy.29
  1252.9 2.1 fusion.132
  1255.0 2.1 fusion.139
  1257.1 1.6 copy.28
  1258.7 1.4 fusion.138
  1260.1 1.4 fusion.130
  1261.5 2.5 fusion.64
  1264.0 1.6 fusion.62
  1265.6 1.8 convolution_subtract_fusion.1
  1267.5 1.7 add_reduce_fusion.1
  1269.2 1.6 convolution_subtract_fusion
  1270.8 1.7 add_reduce_fusion
  1272.7 1.2 fusion.10
  1273.9 1.2 fusion.8
  1275.2 1.3 fusion.19
  1276.5 0.5 fusion.97
  1277.0 0.5 fusion.115
  1277.5 1.2 fusion.2
  1278.7 1.5 fusion
  1280.2 1.3 fusion.31
  1281.5 0.5 fusion.92
  1282.0 0.5 fusion.108
  1282.7 1.2 fusion.25
  1284.0 0.5 convolution_add_fusion.3
  1284.5 0.5 subtract_reduce_fusion.1
  1286.3 1.2 fusion.37
  1287.6 0.5 convolution_add_fusion.2
  1288.1 0.5 subtract_reduce_fusion
  1290.2 0.7 fusion.81
  1292.2 0.9 multiply_reduce_fusion
  1293.2 201.7 %all-reduce = (f32[]{:T(128)}, f32[]{:T(128)}) all-reduce(f32[]{:T(128)} %get-tuple-element.34, f32[]{:T(128)S(6)} %add.285), channel_id=1, replica_groups=mesh['row'=32,'col'=16] {'row','col'}, use_global_device_ids=true, to_apply=%region_7.8 | all-reduce | flops 2 | bytes 16 | tf_op jit(solution)/shard_map/psum | solution.py:120
  1496.2 0.6 divide_subtract_fusion
  (72 shorter events, 8.1 us)
Async XLA Ops:
  2.4 1228.4 %copy-start.13 = (f32[128,128]{1,0:T(8,128)S(1)}, f32[128,128]{1,0:T(8,128)}, u32[]{:S(2)}) copy-start(f32[128,128]{1,0:T(8,128)} %param.6) | copy-start | bytes 196612
  2.4 1228.4 %copy-start.14 = (f32[128,128]{1,0:T(8,128)S(1)}, f32[128,128]{1,0:T(8,128)}, u32[]{:S(2)}) copy-start(f32[128,128]{1,0:T(8,128)} %param.5) | copy-start | bytes 196612
  2.4 1228.4 %collective-permute-start.1 = (f32[3,64,128]{2,1,0:T(8,128)S(1)}, f32[3,64,128]{2,1,0:T(8,128)S(1)}, u32[]{:S(2)}, u32[]{:S(2)}) collective-permute-start(f32[3,64,128]{2,1,0:T(8,128)S(1)} %get-tuple-element.25), channel_id=1, source_target_pairs={{16,0},{32,16},{48,32},{64,48},{80,64},{96,80},{112,96},{128,112},... | collective-permute-start | bytes 294920 | tf_op jit(solution)/shard_map/ppermute | solution.py:29
  11.3 1219.5 %collective-permute-start = (f32[3,64,128]{2,1,0:T(8,128)S(1)}, f32[3,64,128]{2,1,0:T(8,128)S(1)}, u32[]{:S(2)}, u32[]{:S(2)}) collective-permute-start(f32[3,64,128]{2,1,0:T(8,128)S(1)} %get-tuple-element.24), channel_id=1, source_target_pairs={{0,16},{16,32},{32,48},{48,64},{64,80},{80,96},{96,112},{112,128},... | collective-permute-start | bytes 294920 | tf_op jit(solution)/shard_map/ppermute | solution.py:26
  1230.5 13.7 copy-start.9
  1230.6 13.6 copy-start.11
  1230.7 13.5 copy-start.5
  1230.8 13.4 copy-start.7
  1231.1 8.8 collective-permute-start.3
  1232.4 8.7 collective-permute-start.2
  1241.4 0.9 copy-start
  1245.6 1.6 copy-start.4
  1258.7 5.4 copy-start.3
  1267.4 1.7 copy-start.2
  1270.7 1.7 copy-start.1
  1282.7 1.8 copy-start.10
  1282.7 1.8 copy-start.12
  1282.7 2.3 copy-start.17
  1282.7 2.8 copy-start.15
  1285.0 3.1 copy-start.6
  1285.0 3.1 copy-start.8
  1286.3 5.9 copy-start.16
where the time goes:
time: 1500 us
  blocking collectives  1420 us (95%)
  matrix products  44.1 us (3%)
  starting transfers between devices  16.3 us (1%)
    all_gather x1, blocking collectives, shards(): whole_bank = lax.all_gather(kernels, ('row', 'col'), axis=1, tiled=True)  1220 us
    psum x1, blocking collectives, shards(): square_global = lax.psum(square_local, ('row', 'col'))  202 us
    dot_general x42, matrix products, matmul(): jnp.matmul(first, second, precision=lax.Precision.HIGHEST, preferred_elem...  35.1 us
  transfers between devices with their start and end apart: 4, of which 2 were waited for; matrix products, arithmetic and copies ran while one was open for 0% of the time, Pallas kernels for 0%

commit v1 on v0

v1 whole, which is shorter than its diff:
```python
import functools

import numpy as np
import ml_dtypes

import jax
import jax.numpy as jnp
from jax import lax
from jax.experimental import pallas as pl
from jax.experimental.pallas import tpu as pltpu
from jax.sharding import PartitionSpec as P

MESH = pl.DeviceIdType.MESH
F32 = jnp.float32
BF16 = jnp.bfloat16
DOSES = (1.0, 1.15)
EPSILON = 1e-06
CELLS = 4096 * 2048
GRID = 64
ROWS_H = 384


def tables():
    place = np.concatenate([np.arange(64, 192), np.arange(192, 256), np.arange(0, 64)])
    freq = np.arange(32) - 16

    def wave(points):
        turn = 2 * np.pi * ((freq[:, None] * points[None, :]) % 256) / 256
        return np.cos(turn) / 16, np.sin(turn) / 16

    cos_p, sin_p = wave(place)
    cos_g, sin_g = wave(4 * np.arange(GRID))
    out = {}
    mask_re = np.concatenate([cos_p.T, -sin_p.T], 1)
    mask_im = np.concatenate([sin_p.T, cos_p.T], 1)
    out["first"] = np.concatenate([mask_re, mask_re, mask_im, mask_im], 1)
    out["second"] = np.concatenate([cos_p, sin_p], 0)
    line, block = np.divmod(np.arange(ROWS_H), 128)
    core, y, part, low = block // 64, block // 8 % 8, block // 4 % 2, block % 4
    number = 3 * ((y * 2 + core) * 4 + low) + line
    kernel, u = number // 32, number % 32
    out["pick"] = (u[:, None] == np.arange(32)[None, :]).astype(np.float64)
    left_c = np.where(part[:, None] == 0, cos_g[u], -sin_g[u])
    left_d = np.where(part[:, None] == 0, sin_g[u], cos_g[u])
    out["left"] = np.concatenate([left_c, left_d], 0).T
    out["left_t"] = np.concatenate([left_c, left_c, left_d, left_d], 1)
    same = kernel[:, None] == np.arange(6)[None, :]
    out["own"] = np.concatenate([np.tile(same.T, (1, 2)), np.zeros((2, 768))], 0)
    out["own_t"] = np.repeat(same, 64, axis=1).astype(np.float64)
    zero = np.zeros((64, 128))
    right = np.concatenate(
        [np.concatenate([cos_g, sin_g], 1), np.concatenate([-sin_g, cos_g], 1)], 0
    )
    out["right"] = np.concatenate(
        [np.concatenate([right, zero], 1), np.concatenate([zero, right], 1)], 0
    )
    gap = place[:, None] - 4 * np.arange(GRID)[None, :]
    order = np.arange(1, 32)
    spread = (1 + 2 * np.cos(2 * np.pi * (gap[..., None] * order % 256) / 256).sum(-1)) / 64
    out["up_cols"] = np.concatenate([spread.T, spread.T], 0)
    out["up_rows"] = spread
    out["down_rows"] = spread.T
    out["down_cols"] = np.concatenate([spread, spread], 1)
    back = np.concatenate(
        [np.concatenate([cos_g.T, -sin_g.T], 1), np.concatenate([sin_g.T, cos_g.T], 1)], 0
    )
    turned = np.concatenate(
        [np.concatenate([-sin_g.T, -cos_g.T], 1), np.concatenate([cos_g.T, -sin_g.T], 1)], 0
    )
    zero = np.zeros((128, 64))
    out["back"] = np.concatenate(
        [
            np.concatenate([back, zero, turned, zero], 1),
            np.concatenate([zero, back, zero, turned], 1),
        ],
        0,
    )
    cos_c, sin_c = cos_p[:, :128], sin_p[:, :128]
    out["last_rows"] = np.concatenate([cos_c.T[:, u], sin_c.T[:, u]], 0)
    out["last_cols"] = 2 * np.concatenate(
        [cos_c, -sin_c, cos_c, -sin_c, -sin_c, -cos_c, -sin_c, -cos_c], 0
    )
    return out


SPLIT = (
    "first", "second", "right", "up_cols", "up_rows", "down_rows", "down_cols",
    "back", "last_rows", "last_cols",
)
PLAIN = ("left", "left_t", "own", "own_t")


def const_arrays():
    made = tables()
    names, arrays = [], []
    for name in SPLIT:
        value = made[name].astype(np.float32)
        high = value.astype(ml_dtypes.bfloat16)
        low = (value - high.astype(np.float32)).astype(ml_dtypes.bfloat16)
        names += [name + "_hi", name + "_lo"]
        arrays += [high, low]
    for name in PLAIN:
        names.append(name)
        arrays.append(made[name].astype(np.float32))
    names.append("pick")
    arrays.append(made["pick"].astype(ml_dtypes.bfloat16))
    return names, arrays


def split(value):
    high = value.astype(BF16)
    return high, (value - high.astype(F32)).astype(BF16)


def dot(first, second):
    return jnp.dot(first, second, preferred_element_type=F32)


def mm(first, second):
    return dot(first[0], second[0]) + (dot(first[1], second[0]) + dot(first[0], second[1]))


def build_left(k, left, own):
    return split(left * own[k : k + 1, :])


def spectrum(mask, con):
    half = mm(split(mask), con("first"))
    both = mm(con("second"), split(half))
    plain = both[:32, :128] - both[32:, 128:]
    turned = both[:32, 128:] + both[32:, :128]
    high, low = split(jnp.concatenate([plain, turned], axis=1))
    return dot(con.one("pick"), high) + dot(con.one("pick"), low)


def spread_bank(bank):
    lane = lax.broadcasted_iota(jnp.int32, (128, 128), 1)
    out = []
    for line in range(3):
        rolls = []
        for slot in range(4):
            shift = (32 * slot - 32 * line) % 128
            value = bank[slot // 2]
            rolls.append(value if shift == 0 else pltpu.roll(value, shift, 1))
        low = jnp.where(lane < 32, rolls[0], rolls[1])
        high = jnp.where(lane < 96, rolls[2], rolls[3])
        out.append(jnp.where(lane < 64, low, high))
    return jnp.concatenate(out, axis=0)


def fields_of(spec, bank, con, left):
    first = bank * spec[:, :128]
    second = bank * spec[:, 128:]
    lines = mm(left, split(jnp.concatenate([first, second], axis=0)))
    return mm(split(lines), con("right"))


def intensity_of(fields, con):
    square = fields * fields
    total = square[:64]
    for k in range(1, 6):
        total = total + square[64 * k : 64 * k + 64]
    stacked = jnp.concatenate([total[:, :128], total[:, 128:]], axis=0)
    wide = split(mm(split(stacked), con("up_cols")))
    return [mm(con("up_rows"), (wide[0][64 * c : 64 * c + 64], wide[1][64 * c : 64 * c + 64])) for c in range(2)]


def slope_of(intensity, target, weight, dose):
    resist = jax.nn.sigmoid(6.0 * (dose * intensity - 0.75))
    error = resist - target
    scaled = weight * error
    slope = (12.0 * dose) * scaled * resist * (1.0 - resist)
    return slope, (scaled * error)[:128, :128]


def gradient_of(slopes, fields, bank, con, left_t):
    rows = [mm(con("down_rows"), split(slope)) for slope in slopes]
    down = mm(split(jnp.concatenate(rows, axis=0)), con("down_cols"))
    pair = jnp.concatenate([down[:64], down[64:]], axis=1)
    moved = fields * jnp.concatenate([pair] * 6, axis=0)
    lines = mm(split(moved), con("back"))
    stacked = jnp.concatenate([lines[:, :128], lines[:, 128:]], axis=0)
    terms = bank * mm(left_t, split(stacked))
    last = mm(con("last_rows"), split(terms))
    return mm(split(jnp.concatenate([last[:128], last[128:]], axis=1)), con("last_cols"))


class Consts:
    def __init__(self, refs):
        self.refs = refs

    def __call__(self, name):
        return self.refs[name + "_hi"][...], self.refs[name + "_lo"][...]

    def one(self, name):
        return self.refs[name][...]


def kernel(names, *args):
    count = len(names)
    logits_ref, target_ref, weight_ref, bank_ref = args[:4]
    const_hbm = args[4 : 4 + count]
    out_ref, loss_ref = args[4 + count : 6 + count]
    const_vmem = args[6 + count : 6 + 2 * count]
    (
        left_hi, left_lo, left_t_hi, left_t_lo, vert, from_left, from_right,
        x_buf, z_send, z_buf, y_send, h_buf, r_send, r_buf,
        c_sem, vs_sem, vr_sem, hs_sem, hr_sem, es_sem, er_sem,
        xs_sem, xr_sem, zs_sem, zr_sem, ys_sem, yr_sem, rs_sem, rr_sem,
    ) = args[6 + 2 * count :]

    row = lax.axis_index("row")
    col = lax.axis_index("col")
    core = row % 2
    y = row // 2 % 8
    z_hi = row // 16
    z_lo = col // 4
    x = col % 4
    z = z_hi * 4 + z_lo

    def at(z_, y_, core_, x_):
        return ((z_ // 4 * 8 + y_) * 2 + core_, z_ % 4 * 4 + x_)

    x_peers = [at(z, y, core, (x + d) % 4) for d in range(1, 4)]
    xc_peers = [at(z, y, (core + e) % 2, (x + d) % 4) for d in range(4) for e in range(2) if d + e]
    z_peers = [at((z + d) % 8, y, core, x) for d in range(1, 8)]
    yc_peers = [at(z, (y + d) % 8, (core + e) % 2, x) for d in range(8) for e in range(2) if d + e]
    y_peers = [at(z, (y + d) % 8, core, x) for d in range(1, 8)]
    sides = [
        (row > 0, (row - 1, col)),
        (row < 31, (row + 1, col)),
        (col > 0, (row, col - 1)),
        (col < 15, (row, col + 1)),
    ]

    const_copies = [
        pltpu.make_async_copy(const_hbm[i], const_vmem[i], c_sem.at[i]) for i in range(count)
    ]
    for copy in const_copies:
        copy.start()

    for a in range(3):
        value = -1000.0 if a == 0 else 0.0
        vert[a] = jnp.full((128, 128), value, F32)
        from_left[a] = jnp.full((256, 128), value, F32)
        from_right[a] = jnp.full((256, 128), value, F32)

    barrier = pltpu.get_barrier_semaphore()
    for peer in xc_peers + z_peers + yc_peers:
        pl.semaphore_signal(barrier, inc=1, device_id=peer, device_id_type=MESH)
    waits = 29
    for there, peer in sides:
        @pl.when(there)
        def _():
            pl.semaphore_signal(barrier, inc=1, device_id=peer, device_id_type=MESH)
        waits = waits + there.astype(jnp.int32)

    for copy in const_copies:
        copy.wait()
    con = Consts(dict(zip(names, const_vmem)))
    left = con.one("left")
    own = con.one("own")
    for k in range(6):
        high, low = build_left(k, left, own)
        left_hi[64 * k : 64 * k + 64, :] = high
        left_lo[64 * k : 64 * k + 64, :] = low
    for part in range(2):
        table = con.one("left_t")[:, 128 * part : 128 * part + 128]
        for pair in range(3):
            mask = con.one("own_t")[:, 128 * pair : 128 * pair + 128]
            high, low = split(table * mask)
            where = 384 * part + 128 * pair
            left_t_hi[:, where : where + 128] = high
            left_t_lo[:, where : where + 128] = low

    pl.semaphore_wait(barrier, waits)

    def remote(src, dst, send, recv, peer):
        return pltpu.make_async_remote_copy(
            src_ref=src, dst_ref=dst, send_sem=send, recv_sem=recv,
            device_id=peer, device_id_type=MESH,
        )

    x_copies = [
        remote(bank_ref, x_buf.at[x], xs_sem.at[i], xr_sem.at[i], peer)
        for i, peer in enumerate(x_peers)
    ]
    for copy in x_copies:
        copy.start()
    x_buf[x] = bank_ref[...]

    sources = (logits_ref, target_ref, weight_ref)
    v_copies, h_copies, e_copies = [], [], []
    for a in range(3):
        v_copies.append([
            (sides[s][0], sides[1 - s][0], remote(
                sources[a].at[pl.ds(64 * s, 64)], vert.at[a, pl.ds(64 * s, 64)],
                vs_sem.at[a, s], vr_sem.at[a, s], sides[s][1]))
            for s in range(2)
        ])
        h_copies.append([
            (sides[2 + s][0], sides[3 - s][0], remote(
                sources[a], (from_right, from_left)[s].at[a, pl.ds(0, 128)],
                hs_sem.at[a, s], hr_sem.at[a, s], sides[2 + s][1]))
            for s in range(2)
        ])
        e_copies.append([
            (sides[2 + s][0], sides[3 - s][0], remote(
                vert.at[a], (from_right, from_left)[s].at[a, pl.ds(128, 128)],
                es_sem.at[a, s], er_sem.at[a, s], sides[2 + s][1]))
            for s in range(2)
        ])

    def start(group):
        for sends, _, copy in group:
            @pl.when(sends)
            def _():
                copy.start()

    def arrive(group):
        for _, comes, copy in group:
            @pl.when(comes)
            def _():
                copy.wait_recv()

    def sent(group):
        for sends, _, copy in group:
            @pl.when(sends)
            def _():
                copy.wait_send()

    start(v_copies[0])
    start(h_copies[0])
    start(v_copies[1])
    start(v_copies[2])

    for copy in x_copies:
        copy.wait_recv()
    joined = jnp.concatenate(
        [x_buf[0], x_buf[1], x_buf[2], x_buf[3], jnp.zeros((2, 32), F32)], axis=1
    )
    z_send[...] = joined
    z_copies = [
        remote(z_send, z_buf.at[z], zs_sem.at[i], zr_sem.at[i], peer)
        for i, peer in enumerate(z_peers)
    ]
    for copy in z_copies:
        copy.start()
    z_buf[z] = joined

    start(h_copies[1])
    start(h_copies[2])
    arrive(v_copies[0])
    start(e_copies[0])

    for copy in z_copies:
        copy.wait_recv()
    for c in range(2):
        y_send[c] = jnp.concatenate([z_buf[i, c : c + 1, :] for i in range(8)], axis=0)
    mine = core * 8 + y
    y_copies = [
        remote(y_send, h_buf.at[mine], ys_sem.at[i], yr_sem.at[i], peer)
        for i, peer in enumerate(yc_peers)
    ]
    for copy in y_copies:
        copy.start()
    h_buf[mine] = y_send[...]

    for a in (1, 2):
        arrive(v_copies[a])
        start(e_copies[a])

    def padded(a, own_ref):
        first = jnp.concatenate([own_ref[...], vert[a]], axis=0)
        lane = lax.broadcasted_iota(jnp.int32, (256, 128), 1)
        second = jnp.where(lane < 64, from_right[a], from_left[a])
        return jnp.concatenate([first, second], axis=1)

    arrive(h_copies[0])
    arrive(e_copies[0])
    spec = spectrum(jax.nn.sigmoid(padded(0, logits_ref)), con)

    for copy in y_copies:
        copy.wait_recv()
    bank = spread_bank([h_buf[:, c].reshape(128, 128) for c in range(2)])
    fields = fields_of(spec, bank, con, (left_hi[...], left_lo[...]))
    intensity = intensity_of(fields, con)

    for a in (1, 2):
        arrive(h_copies[a])
        arrive(e_copies[a])
    goal = padded(1, target_ref)
    weight = padded(2, weight_ref)
    slopes, losses = [], 0.0
    for c in range(2):
        slope, loss = slope_of(intensity[c], goal, weight, DOSES[c])
        slopes.append(slope)
        losses = losses + loss
    grad = gradient_of(slopes, fields, bank, con, (left_t_hi[...], left_t_lo[...]))
    logits = logits_ref[...]
    mask = jax.nn.sigmoid(logits)
    grad = grad * mask * (1.0 - mask)

    total = jnp.concatenate(
        [jnp.sum(grad * grad, axis=0, keepdims=True), jnp.sum(losses, axis=0, keepdims=True)],
        axis=0,
    )
    slot = 0
    r_copies = []
    for stage, peers in enumerate((xc_peers, z_peers, y_peers)):
        r_send[stage] = total
        copies = [
            remote(r_send.at[stage], r_buf.at[slot + i], rs_sem.at[slot + i], rr_sem.at[slot + i], peer)
            for i, peer in enumerate(peers)
        ]
        for copy in copies:
            copy.start()
        for copy in copies:
            copy.wait_recv()
        for i in range(len(peers)):
            total = total + r_buf[slot + i]
        slot += len(peers)
        r_copies += copies

    squares = jnp.sum(total[0:1, :], axis=1, keepdims=True)
    loss_ref[0, 0] = jnp.sum(total[1:2, :]) / CELLS
    norm = jnp.sqrt(squares / CELLS + EPSILON)
    out_ref[...] = logits - 0.5 * grad / norm

    for a in range(3):
        sent(v_copies[a])
        sent(h_copies[a])
        sent(e_copies[a])
    for copy in x_copies + z_copies + y_copies + r_copies:
        copy.wait_send()


def shards(mask_logits, target, weight, kernels):
    names, arrays = const_arrays()
    count = len(names)
    vmem = pl.BlockSpec(memory_space=pltpu.VMEM)
    dma = pltpu.SemaphoreType.DMA
    scratch = [pltpu.VMEM(a.shape, a.dtype) for a in arrays] + [
        pltpu.VMEM((384, 768), BF16), pltpu.VMEM((384, 768), BF16),
        pltpu.VMEM((384, 768), BF16), pltpu.VMEM((384, 768), BF16),
        pltpu.VMEM((3, 128, 128), F32),
        pltpu.VMEM((3, 256, 128), F32), pltpu.VMEM((3, 256, 128), F32),
        pltpu.VMEM((4, 2, 24), F32),
        pltpu.VMEM((2, 128), F32), pltpu.VMEM((8, 2, 128), F32),
        pltpu.VMEM((2, 8, 128), F32), pltpu.VMEM((16, 2, 8, 128), F32),
        pltpu.VMEM((3, 2, 128), F32), pltpu.VMEM((21, 2, 128), F32),
        dma((count,)), dma((3, 2)), dma((3, 2)), dma((3, 2)), dma((3, 2)), dma((3, 2)), dma((3, 2)),
        dma((3,)), dma((3,)), dma((7,)), dma((7,)), dma((15,)), dma((15,)), dma((21,)), dma((21,)),
    ]
    new_logits, loss = pl.pallas_call(
        functools.partial(kernel, names),
        out_shape=(
            jax.ShapeDtypeStruct((128, 128), F32),
            jax.ShapeDtypeStruct((1, 1), F32),
        ),
        in_specs=[vmem] * 4 + [pl.BlockSpec(memory_space=pl.ANY)] * count,
        out_specs=(vmem, pl.BlockSpec(memory_space=pltpu.SMEM)),
        scratch_shapes=scratch,
        compiler_params=pltpu.CompilerParams(collective_id=0, has_side_effects=True),
        name="litho",
    )(mask_logits, target, weight, kernels, *[jnp.asarray(a) for a in arrays])
    return new_logits, loss.reshape(())


def solution(mesh):
    placed = (P("row", "col"), P("row", "col"), P("row", "col"), P(None, ("row", "col")))
    return jax.shard_map(
        shards, mesh=mesh, in_specs=placed, out_specs=(P("row", "col"), P()), check_vma=False
    )
```

time: 1500 us -> 52 us (0.03)
  blocking collectives: 1420 us -> 0 us
  Pallas kernels: 0 us -> 47.9 us
  matrix products: 44.1 us -> 0 us
  starting transfers between devices: 16.3 us -> 0 us
    all_gather x1 -> x0, blocking collectives: 1220 us -> none  [shards(): whole_bank = lax.all_gather(kernels, ('row', 'col'), axis=1, tiled=True)]
    psum x1 -> x0, blocking collectives: 202 us -> none  [shards(): square_global = lax.psum(square_local, ('row', 'col'))]
    pallas_call x0 -> x1, Pallas kernels: none -> 47.9 us  [shards(): pl.pallas_call(functools.partial(kernel, names), out_shape=(jax.ShapeDtyp...]
    dot_general x42 -> x0, matrix products: 35.1 us -> none  [matmul(): jnp.matmul(first, second, precision=lax.Precision.HIGHEST, preferred_elem...]
    ppermute x4 -> x0, starting transfers between devices: 16.3 us -> none  [the longest x2 10.2 us: padded_2(): lax.ppermute(lax.slice_in_dim(block, 0, width, axis=dim), axis, backward)]
  transfers between devices with their start and end apart: 4 -> 0, of which waited for: 2 -> 0; matrix products, arithmetic and copies ran while one was open for 0% -> 0% of each run, Pallas kernels for 0% -> 0%
where the time goes in v1:
time: 52 us; the launch traced here: 51.8 us
  Pallas kernels  47.9 us (92%)
  between operations  2.39 us (5%)
  local copies, waits for them, and re-layouts  1.47 us (3%)
    pallas_call x1, Pallas kernels, shards(): pl.pallas_call(functools.partial(kernel, names), out_shape=(jax.ShapeDtyp...  47.9 us
    unnamed x1, local copies, waits for them, and re-layouts  1.47 us

profile of v1, /device:TPU:1, one launch (start us, length us, event | category | flops | bytes accessed | tf_op | source)
XLA Modules:
  0.0 51.8 jit_solution(259018687036434371)
XLA Ops:
  0.6 47.9 %litho.1 = (f32[128,128]{1,0:T(8,128)}, f32[1,1]{1,0:T(1,128)}) custom-call(f32[128,128]{1,0:T(8,128)} %args_0_.4, f32[128,128]{1,0:T(8,128)} %args_1_.4, f32[128,128]{1,0:T(8,128)} %args_2_.4, f32[2,24]{1,0:T(2,128)} %args_3_.4, bf16[256,256]{1,0:T(8,128)(2,1)} %constant.50.clone.args_4_, bf16[256,256]{1,0:T(8,128)(2,1)} %constant.51.clone.args_5_, ...), custom_call_target="tpu_custom_call" | custom-call | tf_op jit(solution)/shard_map/litho/pallas_call | solution.py:455
  48.5 1.5 %copy.33 = f32[128,128]{1,0:T(8,128)} copy(f32[128,128]{1,0:T(8,128)} %get-tuple-element.8) | data formatting | bytes 131072

commit v2 on v1

--- a/solution.py
+++ b/solution.py
@@ -204,9 +204,9 @@
     const_vmem = args[6 + count : 6 + 2 * count]
     (
         left_hi, left_lo, left_t_hi, left_t_lo, vert, from_left, from_right,
-        x_buf, z_send, z_buf, y_send, h_buf, r_send, r_buf,
+        x_buf, y_send, h_buf, r_send, r_buf,
         c_sem, vs_sem, vr_sem, hs_sem, hr_sem, es_sem, er_sem,
-        xs_sem, xr_sem, zs_sem, zr_sem, ys_sem, yr_sem, rs_sem, rr_sem,
+        xs_sem, xr_sem, ys_sem, yr_sem, ps_sem, pr_sem, rs_sem, rr_sem,
     ) = args[6 + 2 * count :]
 
     row = lax.axis_index("row")
@@ -221,10 +221,12 @@
     def at(z_, y_, core_, x_):
         return ((z_ // 4 * 8 + y_) * 2 + core_, z_ % 4 * 4 + x_)
 
-    x_peers = [at(z, y, core, (x + d) % 4) for d in range(1, 4)]
-    xc_peers = [at(z, y, (core + e) % 2, (x + d) % 4) for d in range(4) for e in range(2) if d + e]
-    z_peers = [at((z + d) % 8, y, core, x) for d in range(1, 8)]
-    yc_peers = [at(z, (y + d) % 8, (core + e) % 2, x) for d in range(8) for e in range(2) if d + e]
+    partner = at(z, y, 1 - core, x)
+    xz_peers = [at((z + d) % 8, y, core, (x + e) % 4) for d in range(8) for e in range(4) if d + e]
+    xzc_peers = [
+        at((z + d) % 8, y, (core + f) % 2, (x + e) % 4)
+        for d in range(8) for e in range(4) for f in range(2) if d + e + f
+    ]
     y_peers = [at(z, (y + d) % 8, core, x) for d in range(1, 8)]
     sides = [
         (row > 0, (row - 1, col)),
@@ -233,45 +235,35 @@
         (col < 15, (row, col + 1)),
     ]
 
-    const_copies = [
-        pltpu.make_async_copy(const_hbm[i], const_vmem[i], c_sem.at[i]) for i in range(count)
-    ]
-    for copy in const_copies:
-        copy.start()
-
-    for a in range(3):
-        value = -1000.0 if a == 0 else 0.0
-        vert[a] = jnp.full((128, 128), value, F32)
-        from_left[a] = jnp.full((256, 128), value, F32)
-        from_right[a] = jnp.full((256, 128), value, F32)
-
     barrier = pltpu.get_barrier_semaphore()
-    for peer in xc_peers + z_peers + yc_peers:
+    for peer in [partner] + xz_peers + y_peers:
         pl.semaphore_signal(barrier, inc=1, device_id=peer, device_id_type=MESH)
-    waits = 29
+    waits = 39
     for there, peer in sides:
         @pl.when(there)
         def _():
             pl.semaphore_signal(barrier, inc=1, device_id=peer, device_id_type=MESH)
         waits = waits + there.astype(jnp.int32)
 
+    const_copies = [
+        pltpu.make_async_copy(const_hbm[i], const_vmem[i], c_sem.at[i]) for i in range(count)
+    ]
     for copy in const_copies:
-        copy.wait()
-    con = Consts(dict(zip(names, const_vmem)))
-    left = con.one("left")
-    own = con.one("own")
-    for k in range(6):
-        high, low = build_left(k, left, own)
-        left_hi[64 * k : 64 * k + 64, :] = high
-        left_lo[64 * k : 64 * k + 64, :] = low
-    for part in range(2):
-        table = con.one("left_t")[:, 128 * part : 128 * part + 128]
-        for pair in range(3):
-            mask = con.one("own_t")[:, 128 * pair : 128 * pair + 128]
-            high, low = split(table * mask)
-            where = 384 * part + 128 * pair
-            left_t_hi[:, where : where + 128] = high
-            left_t_lo[:, where : where + 128] = low
+        copy.start()
+
+    def fill(ref):
+        ref[...] = jnp.zeros(ref.shape, F32)
+        ref[0] = jnp.full(ref.shape[1:], -1000.0, F32)
+
+    for missing, ref in (
+        (row == 0, vert.at[:, pl.ds(64, 64)]),
+        (row == 31, vert.at[:, pl.ds(0, 64)]),
+        (col == 0, from_left),
+        (col == 15, from_right),
+    ):
+        @pl.when(missing)
+        def _():
+            fill(ref)
 
     pl.semaphore_wait(barrier, waits)
 
@@ -282,12 +274,12 @@
         )
 
     x_copies = [
-        remote(bank_ref, x_buf.at[x], xs_sem.at[i], xr_sem.at[i], peer)
-        for i, peer in enumerate(x_peers)
+        remote(bank_ref, x_buf.at[z, x], xs_sem.at[i], xr_sem.at[i], peer)
+        for i, peer in enumerate(xz_peers)
     ]
     for copy in x_copies:
         copy.start()
-    x_buf[x] = bank_ref[...]
+    x_buf[z, x] = bank_ref[...]
 
     sources = (logits_ref, target_ref, weight_ref)
     v_copies, h_copies, e_copies = [], [], []
@@ -333,38 +325,53 @@
     start(h_copies[0])
     start(v_copies[1])
     start(v_copies[2])
+    start(h_copies[1])
+    start(h_copies[2])
+
+    for copy in const_copies:
+        copy.wait()
+    con = Consts(dict(zip(names, const_vmem)))
+    left = con.one("left")
+    own = con.one("own")
+    for k in range(6):
+        high, low = build_left(k, left, own)
+        left_hi[64 * k : 64 * k + 64, :] = high
+        left_lo[64 * k : 64 * k + 64, :] = low
+    for part in range(2):
+        table = con.one("left_t")[:, 128 * part : 128 * part + 128]
+        for pair in range(3):
+            mask = con.one("own_t")[:, 128 * pair : 128 * pair + 128]
+            high, low = split(table * mask)
+            where = 384 * part + 128 * pair
+            left_t_hi[:, where : where + 128] = high
+            left_t_lo[:, where : where + 128] = low
 
     for copy in x_copies:
         copy.wait_recv()
-    joined = jnp.concatenate(
-        [x_buf[0], x_buf[1], x_buf[2], x_buf[3], jnp.zeros((2, 32), F32)], axis=1
-    )
-    z_send[...] = joined
-    z_copies = [
-        remote(z_send, z_buf.at[z], zs_sem.at[i], zr_sem.at[i], peer)
-        for i, peer in enumerate(z_peers)
-    ]
-    for copy in z_copies:
-        copy.start()
-    z_buf[z] = joined
-
-    start(h_copies[1])
-    start(h_copies[2])
-    arrive(v_copies[0])
-    start(e_copies[0])
-
-    for copy in z_copies:
-        copy.wait_recv()
     for c in range(2):
-        y_send[c] = jnp.concatenate([z_buf[i, c : c + 1, :] for i in range(8)], axis=0)
+        parts = [
+            jnp.concatenate([x_buf[i, p, c : c + 1, :] for i in range(8)], axis=0)
+            for p in range(4)
+        ]
+        y_send[c] = jnp.concatenate(parts + [jnp.zeros((8, 32), F32)], axis=1)
     mine = core * 8 + y
     y_copies = [
         remote(y_send, h_buf.at[mine], ys_sem.at[i], yr_sem.at[i], peer)
-        for i, peer in enumerate(yc_peers)
+        for i, peer in enumerate(y_peers)
     ]
     for copy in y_copies:
         copy.start()
+    p_copies = [remote(y_send, h_buf.at[mine], ps_sem.at[0], pr_sem.at[0], partner)]
+    p_copies[0].start()
     h_buf[mine] = y_send[...]
+
+    arrive(v_copies[0])
+    start(e_copies[0])
+    for i in (0, 6, 1, 5, 2, 4, 3):
+        y_copies[i].wait_recv()
+        piece = h_buf.at[core * 8 + (y + 7 - i) % 8]
+        p_copies.append(remote(piece, piece, ps_sem.at[1 + i], pr_sem.at[1 + i], partner))
+        p_copies[-1].start()
 
     for a in (1, 2):
         arrive(v_copies[a])
@@ -380,7 +387,7 @@
     arrive(e_copies[0])
     spec = spectrum(jax.nn.sigmoid(padded(0, logits_ref)), con)
 
-    for copy in y_copies:
+    for copy in p_copies:
         copy.wait_recv()
     bank = spread_bank([h_buf[:, c].reshape(128, 128) for c in range(2)])
     fields = fields_of(spec, bank, con, (left_hi[...], left_lo[...]))
@@ -407,7 +414,7 @@
     )
     slot = 0
     r_copies = []
-    for stage, peers in enumerate((xc_peers, z_peers, y_peers)):
+    for stage, peers in enumerate((xzc_peers, y_peers)):
         r_send[stage] = total
         copies = [
             remote(r_send.at[stage], r_buf.at[slot + i], rs_sem.at[slot + i], rr_sem.at[slot + i], peer)
@@ -431,7 +438,7 @@
         sent(v_copies[a])
         sent(h_copies[a])
         sent(e_copies[a])
-    for copy in x_copies + z_copies + y_copies + r_copies:
+    for copy in x_copies + y_copies + p_copies + r_copies:
         copy.wait_send()
 
 
@@ -445,12 +452,11 @@
         pltpu.VMEM((384, 768), BF16), pltpu.VMEM((384, 768), BF16),
         pltpu.VMEM((3, 128, 128), F32),
         pltpu.VMEM((3, 256, 128), F32), pltpu.VMEM((3, 256, 128), F32),
-        pltpu.VMEM((4, 2, 24), F32),
-        pltpu.VMEM((2, 128), F32), pltpu.VMEM((8, 2, 128), F32),
+        pltpu.VMEM((8, 4, 2, 24), F32),
         pltpu.VMEM((2, 8, 128), F32), pltpu.VMEM((16, 2, 8, 128), F32),
-        pltpu.VMEM((3, 2, 128), F32), pltpu.VMEM((21, 2, 128), F32),
+        pltpu.VMEM((2, 2, 128), F32), pltpu.VMEM((70, 2, 128), F32),
         dma((count,)), dma((3, 2)), dma((3, 2)), dma((3, 2)), dma((3, 2)), dma((3, 2)), dma((3, 2)),
-        dma((3,)), dma((3,)), dma((7,)), dma((7,)), dma((15,)), dma((15,)), dma((21,)), dma((21,)),
+        dma((31,)), dma((31,)), dma((7,)), dma((7,)), dma((8,)), dma((8,)), dma((70,)), dma((70,)),
     ]
     new_logits, loss = pl.pallas_call(
         functools.partial(kernel, names),

time: 52 us -> 52.4 us (level)
  no operation moved by 1% of the time
where the time goes in v2:
time: 52.4 us; the launch traced here: 52.2 us
  Pallas kernels  48.3 us (92%)
  between operations  2.39 us (5%)
  local copies, waits for them, and re-layouts  1.47 us (3%)
    pallas_call x1, Pallas kernels, shards(): pl.pallas_call(functools.partial(kernel, names), out_shape=(jax.ShapeDtyp...  48.3 us
    unnamed x1, local copies, waits for them, and re-layouts  1.47 us

profile of v2, /device:TPU:1, one launch (start us, length us, event | category | flops | bytes accessed | tf_op | source)
XLA Modules:
  0.0 52.2 jit_solution(13348769074020285571)
XLA Ops:
  0.6 48.3 %litho.1 = (f32[128,128]{1,0:T(8,128)}, f32[1,1]{1,0:T(1,128)}) custom-call(f32[128,128]{1,0:T(8,128)} %args_0_.4, f32[128,128]{1,0:T(8,128)} %args_1_.4, f32[128,128]{1,0:T(8,128)} %args_2_.4, f32[2,24]{1,0:T(2,128)} %args_3_.4, bf16[256,256]{1,0:T(8,128)(2,1)} %constant.50.clone.args_4_, bf16[256,256]{1,0:T(8,128)(2,1)} %constant.51.clone.args_5_, ...), custom_call_target="tpu_custom_call" | custom-call | tf_op jit(solution)/shard_map/litho/pallas_call | solution.py:461
  49.0 1.5 %copy.33 = f32[128,128]{1,0:T(8,128)} copy(f32[128,128]{1,0:T(8,128)} %get-tuple-element.8) | data formatting | bytes 131072

commit v3 on v2

--- a/solution.py
+++ b/solution.py
@@ -203,10 +203,10 @@
     out_ref, loss_ref = args[4 + count : 6 + count]
     const_vmem = args[6 + count : 6 + 2 * count]
     (
-        left_hi, left_lo, left_t_hi, left_t_lo, vert, from_left, from_right,
+        left_hi, left_lo, left_t_hi, left_t_lo, vert, pack, from_left, from_right,
         x_buf, y_send, h_buf, r_send, r_buf,
         c_sem, vs_sem, vr_sem, hs_sem, hr_sem, es_sem, er_sem,
-        xs_sem, xr_sem, ys_sem, yr_sem, ps_sem, pr_sem, rs_sem, rr_sem,
+        xs_sem, xr_sem, ys_sem, yr_sem, rs_sem, rr_sem,
     ) = args[6 + 2 * count :]
 
     row = lax.axis_index("row")
@@ -221,13 +221,8 @@
     def at(z_, y_, core_, x_):
         return ((z_ // 4 * 8 + y_) * 2 + core_, z_ % 4 * 4 + x_)
 
-    partner = at(z, y, 1 - core, x)
     xz_peers = [at((z + d) % 8, y, core, (x + e) % 4) for d in range(8) for e in range(4) if d + e]
-    xzc_peers = [
-        at((z + d) % 8, y, (core + f) % 2, (x + e) % 4)
-        for d in range(8) for e in range(4) for f in range(2) if d + e + f
-    ]
-    y_peers = [at(z, (y + d) % 8, core, x) for d in range(1, 8)]
+    yc_peers = [at(z, (y + d) % 8, (core + e) % 2, x) for d in range(8) for e in range(2) if d + e]
     sides = [
         (row > 0, (row - 1, col)),
         (row < 31, (row + 1, col)),
@@ -236,9 +231,9 @@
     ]
 
     barrier = pltpu.get_barrier_semaphore()
-    for peer in [partner] + xz_peers + y_peers:
+    for peer in xz_peers + yc_peers:
         pl.semaphore_signal(barrier, inc=1, device_id=peer, device_id_type=MESH)
-    waits = 39
+    waits = 46
     for there, peer in sides:
         @pl.when(there)
         def _():
@@ -251,19 +246,48 @@
     for copy in const_copies:
         copy.start()
 
-    def fill(ref):
-        ref[...] = jnp.zeros(ref.shape, F32)
-        ref[0] = jnp.full(ref.shape[1:], -1000.0, F32)
-
-    for missing, ref in (
-        (row == 0, vert.at[:, pl.ds(64, 64)]),
-        (row == 31, vert.at[:, pl.ds(0, 64)]),
-        (col == 0, from_left),
-        (col == 15, from_right),
+    def fill_rows(first):
+        vert[0, first : first + 64] = jnp.full((64, 128), -1000.0, F32)
+        for a in (1, 2):
+            vert[a, first : first + 64] = jnp.zeros((64, 128), F32)
+
+    def fill_side(ref):
+        ref[0:128] = jnp.full((128, 128), -1000.0, F32)
+        ref[128:384] = jnp.zeros((256, 128), F32)
+
+    for missing, fill, where in (
+        (row == 0, fill_rows, 64),
+        (row == 31, fill_rows, 0),
+        (col == 0, fill_side, from_left),
+        (col == 15, fill_side, from_right),
     ):
         @pl.when(missing)
         def _():
-            fill(ref)
+            fill(where)
+
+    low_lanes = lax.broadcasted_iota(jnp.int32, (64, 128), 1) < 64
+    low_pair = lax.broadcasted_iota(jnp.int32, (128, 128), 1) < 64
+
+    def pack_logits(block, line):
+        top, bottom = block[:64], block[64:]
+        pack[0, line : line + 64] = jnp.where(low_lanes, top, pltpu.roll(bottom, 64, 1))
+        pack[1, line : line + 64] = jnp.where(low_lanes, pltpu.roll(top, 64, 1), bottom)
+
+    def unfolded(block):
+        core_rows, margin = block[:64], block[64:]
+        return [core_rows, pltpu.roll(core_rows, 64, 1), margin, pltpu.roll(margin, 64, 1)]
+
+    def unfolded_high(block):
+        core_rows, margin = block[:64], block[64:]
+        return [pltpu.roll(core_rows, 64, 1), core_rows, pltpu.roll(margin, 64, 1), margin]
+
+    def pack_pair(first, second, line):
+        line = line + 128
+        pack[0, line : line + 128] = jnp.where(low_pair, first, pltpu.roll(second, 64, 1))
+        pack[1, line : line + 128] = jnp.where(low_pair, pltpu.roll(first, 64, 1), second)
+
+    pack_logits(logits_ref[...], 0)
+    pack_pair(target_ref[...], weight_ref[...], 0)
 
     pl.semaphore_wait(barrier, waits)
 
@@ -282,26 +306,31 @@
     x_buf[z, x] = bank_ref[...]
 
     sources = (logits_ref, target_ref, weight_ref)
-    v_copies, h_copies, e_copies = [], [], []
-    for a in range(3):
-        v_copies.append([
+    v_copies = [
+        [
             (sides[s][0], sides[1 - s][0], remote(
                 sources[a].at[pl.ds(64 * s, 64)], vert.at[a, pl.ds(64 * s, 64)],
                 vs_sem.at[a, s], vr_sem.at[a, s], sides[s][1]))
             for s in range(2)
-        ])
-        h_copies.append([
+        ]
+        for a in range(3)
+    ]
+
+    def side_copies(lines, send, recv):
+        return [
             (sides[2 + s][0], sides[3 - s][0], remote(
-                sources[a], (from_right, from_left)[s].at[a, pl.ds(0, 128)],
-                hs_sem.at[a, s], hr_sem.at[a, s], sides[2 + s][1]))
+                pack.at[s, lines], (from_right, from_left)[s].at[lines],
+                send.at[s], recv.at[s], sides[2 + s][1]))
             for s in range(2)
-        ])
-        e_copies.append([
-            (sides[2 + s][0], sides[3 - s][0], remote(
-                vert.at[a], (from_right, from_left)[s].at[a, pl.ds(128, 128)],
-                es_sem.at[a, s], er_sem.at[a, s], sides[2 + s][1]))
-            for s in range(2)
-        ])
+        ]
+
+    h_copies = [
+        side_copies(pl.ds(64 * (2 * a), 64 * (a + 1)), hs_sem.at[a], hr_sem.at[a]) for a in range(2)
+    ]
+    e_copies = [
+        side_copies(pl.ds(64 * (3 * a + 1), 64 * (a + 1)), es_sem.at[a], er_sem.at[a])
+        for a in range(2)
+    ]
 
     def start(group):
         for sends, _, copy in group:
@@ -326,7 +355,6 @@
     start(v_copies[1])
     start(v_copies[2])
     start(h_copies[1])
-    start(h_copies[2])
 
     for copy in const_copies:
         copy.wait()
@@ -357,54 +385,65 @@
     mine = core * 8 + y
     y_copies = [
         remote(y_send, h_buf.at[mine], ys_sem.at[i], yr_sem.at[i], peer)
-        for i, peer in enumerate(y_peers)
+        for i, peer in enumerate(yc_peers)
     ]
     for copy in y_copies:
         copy.start()
-    p_copies = [remote(y_send, h_buf.at[mine], ps_sem.at[0], pr_sem.at[0], partner)]
-    p_copies[0].start()
     h_buf[mine] = y_send[...]
 
     arrive(v_copies[0])
+    pack_logits(vert[0], 64)
     start(e_copies[0])
-    for i in (0, 6, 1, 5, 2, 4, 3):
-        y_copies[i].wait_recv()
-        piece = h_buf.at[core * 8 + (y + 7 - i) % 8]
-        p_copies.append(remote(piece, piece, ps_sem.at[1 + i], pr_sem.at[1 + i], partner))
-        p_copies[-1].start()
-
-    for a in (1, 2):
-        arrive(v_copies[a])
-        start(e_copies[a])
-
-    def padded(a, own_ref):
-        first = jnp.concatenate([own_ref[...], vert[a]], axis=0)
-        lane = lax.broadcasted_iota(jnp.int32, (256, 128), 1)
-        second = jnp.where(lane < 64, from_right[a], from_left[a])
-        return jnp.concatenate([first, second], axis=1)
+    arrive(v_copies[1])
+    arrive(v_copies[2])
+    pack_pair(vert[1], vert[2], 128)
+    start(e_copies[1])
 
     arrive(h_copies[0])
     arrive(e_copies[0])
-    spec = spectrum(jax.nn.sigmoid(padded(0, logits_ref)), con)
-
-    for copy in p_copies:
+    fold_right = jnp.concatenate(unfolded(from_right[0:128]), axis=0)
+    fold_left = jnp.concatenate(unfolded_high(from_left[0:128]), axis=0)
+    logits = logits_ref[...]
+    lane = lax.broadcasted_iota(jnp.int32, (256, 128), 1)
+    wide = jnp.concatenate(
+        [
+            jnp.concatenate([logits, vert[0]], axis=0),
+            jnp.where(lane < 64, fold_right, fold_left),
+        ],
+        axis=1,
+    )
+    spec = spectrum(jax.nn.sigmoid(wide), con)
+
+    for copy in y_copies:
         copy.wait_recv()
     bank = spread_bank([h_buf[:, c].reshape(128, 128) for c in range(2)])
     fields = fields_of(spec, bank, con, (left_hi[...], left_lo[...]))
     intensity = intensity_of(fields, con)
 
-    for a in (1, 2):
-        arrive(h_copies[a])
-        arrive(e_copies[a])
-    goal = padded(1, target_ref)
-    weight = padded(2, weight_ref)
+    arrive(h_copies[1])
+    arrive(e_copies[1])
+    pair_right = from_right[128:384]
+    pair_left = from_left[128:384]
+    goal = jnp.concatenate(
+        [
+            jnp.concatenate([target_ref[...], vert[1]], axis=0),
+            jnp.where(lane < 64, pair_right, pltpu.roll(pair_left, 64, 1)),
+        ],
+        axis=1,
+    )
+    weight = jnp.concatenate(
+        [
+            jnp.concatenate([weight_ref[...], vert[2]], axis=0),
+            jnp.where(lane < 64, pltpu.roll(pair_right, 64, 1), pair_left),
+        ],
+        axis=1,
+    )
     slopes, losses = [], 0.0
     for c in range(2):
         slope, loss = slope_of(intensity[c], goal, weight, DOSES[c])
         slopes.append(slope)
         losses = losses + loss
     grad = gradient_of(slopes, fields, bank, con, (left_t_hi[...], left_t_lo[...]))
-    logits = logits_ref[...]
     mask = jax.nn.sigmoid(logits)
     grad = grad * mask * (1.0 - mask)
 
@@ -414,7 +453,7 @@
     )
     slot = 0
     r_copies = []
-    for stage, peers in enumerate((xzc_peers, y_peers)):
+    for stage, peers in enumerate((xz_peers, yc_peers)):
         r_send[stage] = total
         copies = [
             remote(r_send.at[stage], r_buf.at[slot + i], rs_sem.at[slot + i], rr_sem.at[slot + i], peer)
@@ -434,11 +473,9 @@
     norm = jnp.sqrt(squares / CELLS + EPSILON)
     out_ref[...] = logits - 0.5 * grad / norm
 
-    for a in range(3):
-        sent(v_copies[a])
-        sent(h_copies[a])
-        sent(e_copies[a])
-    for copy in x_copies + y_copies + p_copies + r_copies:
+    for group in v_copies + h_copies + e_copies:
+        sent(group)
+    for copy in x_copies + y_copies + r_copies:
         copy.wait_send()
 
 
@@ -451,12 +488,12 @@
         pltpu.VMEM((384, 768), BF16), pltpu.VMEM((384, 768), BF16),
         pltpu.VMEM((384, 768), BF16), pltpu.VMEM((384, 768), BF16),
         pltpu.VMEM((3, 128, 128), F32),
-        pltpu.VMEM((3, 256, 128), F32), pltpu.VMEM((3, 256, 128), F32),
+        pltpu.VMEM((2, 384, 128), F32), pltpu.VMEM((384, 128), F32), pltpu.VMEM((384, 128), F32),
         pltpu.VMEM((8, 4, 2, 24), F32),
         pltpu.VMEM((2, 8, 128), F32), pltpu.VMEM((16, 2, 8, 128), F32),
-        pltpu.VMEM((2, 2, 128), F32), pltpu.VMEM((70, 2, 128), F32),
-        dma((count,)), dma((3, 2)), dma((3, 2)), dma((3, 2)), dma((3, 2)), dma((3, 2)), dma((3, 2)),
-        dma((31,)), dma((31,)), dma((7,)), dma((7,)), dma((8,)), dma((8,)), dma((70,)), dma((70,)),
+        pltpu.VMEM((2, 2, 128), F32), pltpu.VMEM((46, 2, 128), F32),
+        dma((count,)), dma((3, 2)), dma((3, 2)), dma((2, 2)), dma((2, 2)), dma((2, 2)), dma((2, 2)),
+        dma((31,)), dma((31,)), dma((15,)), dma((15,)), dma((46,)), dma((46,)),
     ]
     new_logits, loss = pl.pallas_call(
         functools.partial(kernel, names),

time: 52.4 us -> 50.6 us (0.966)
  Pallas kernels: 48.3 us -> 46.5 us
    pallas_call x1, Pallas kernels: 48.3 us -> 46.5 us  [shards(): pl.pallas_call(functools.partial(kernel, names), out_shape=(jax.ShapeDtyp...]
where the time goes in v3:
time: 50.6 us; the launch traced here: 50.3 us
  Pallas kernels  46.5 us (92%)
  between operations  2.39 us (5%)
  local copies, waits for them, and re-layouts  1.47 us (3%)
    pallas_call x1, Pallas kernels, shards(): pl.pallas_call(functools.partial(kernel, names), out_shape=(jax.ShapeDtyp...  46.5 us
    unnamed x1, local copies, waits for them, and re-layouts  1.47 us

profile of v3, /device:TPU:1, one launch (start us, length us, event | category | flops | bytes accessed | tf_op | source)
XLA Modules:
  0.0 50.3 jit_solution(9092494801448475989)
XLA Ops:
  0.6 46.5 %litho.1 = (f32[128,128]{1,0:T(8,128)}, f32[1,1]{1,0:T(1,128)}) custom-call(f32[128,128]{1,0:T(8,128)} %args_0_.4, f32[128,128]{1,0:T(8,128)} %args_1_.4, f32[128,128]{1,0:T(8,128)} %args_2_.4, f32[2,24]{1,0:T(2,128)} %args_3_.4, bf16[256,256]{1,0:T(8,128)(2,1)} %constant.50.clone.args_4_, bf16[256,256]{1,0:T(8,128)(2,1)} %constant.51.clone.args_5_, ...), custom_call_target="tpu_custom_call" | custom-call | tf_op jit(solution)/shard_map/litho/pallas_call | solution.py:498
  47.1 1.5 %copy.33 = f32[128,128]{1,0:T(8,128)} copy(f32[128,128]{1,0:T(8,128)} %get-tuple-element.8) | data formatting | bytes 131072

commit v4 on v3

--- a/solution.py
+++ b/solution.py
@@ -198,14 +198,15 @@
 
 def kernel(names, *args):
     count = len(names)
-    logits_ref, target_ref, weight_ref, bank_ref = args[:4]
+    inputs_hbm = args[:4]
     const_hbm = args[4 : 4 + count]
     out_ref, loss_ref = args[4 + count : 6 + count]
     const_vmem = args[6 + count : 6 + 2 * count]
     (
+        logits_ref, target_ref, weight_ref, bank_ref,
         left_hi, left_lo, left_t_hi, left_t_lo, vert, pack, from_left, from_right,
         x_buf, y_send, h_buf, r_send, r_buf,
-        c_sem, vs_sem, vr_sem, hs_sem, hr_sem, es_sem, er_sem,
+        i_sem, c_sem, vs_sem, vr_sem, hs_sem, hr_sem, es_sem, er_sem,
         xs_sem, xr_sem, ys_sem, yr_sem, rs_sem, rr_sem,
     ) = args[6 + 2 * count :]
 
@@ -240,6 +241,12 @@
             pl.semaphore_signal(barrier, inc=1, device_id=peer, device_id_type=MESH)
         waits = waits + there.astype(jnp.int32)
 
+    inputs = (logits_ref, target_ref, weight_ref, bank_ref)
+    input_copies = [
+        pltpu.make_async_copy(inputs_hbm[i], inputs[i], i_sem.at[i]) for i in range(4)
+    ]
+    for copy in input_copies:
+        copy.start()
     const_copies = [
         pltpu.make_async_copy(const_hbm[i], const_vmem[i], c_sem.at[i]) for i in range(count)
     ]
@@ -286,6 +293,8 @@
         pack[0, line : line + 128] = jnp.where(low_pair, first, pltpu.roll(second, 64, 1))
         pack[1, line : line + 128] = jnp.where(low_pair, pltpu.roll(first, 64, 1), second)
 
+    for copy in input_copies:
+        copy.wait()
     pack_logits(logits_ref[...], 0)
     pack_pair(target_ref[...], weight_ref[...], 0)
 
@@ -469,7 +478,8 @@
         r_copies += copies
 
     squares = jnp.sum(total[0:1, :], axis=1, keepdims=True)
-    loss_ref[0, 0] = jnp.sum(total[1:2, :]) / CELLS
+    loss = jnp.sum(total[1:2, :], axis=1, keepdims=True) / CELLS
+    loss_ref[...] = jnp.broadcast_to(loss, (1, 128))
     norm = jnp.sqrt(squares / CELLS + EPSILON)
     out_ref[...] = logits - 0.5 * grad / norm
 
@@ -485,6 +495,8 @@
     vmem = pl.BlockSpec(memory_space=pltpu.VMEM)
     dma = pltpu.SemaphoreType.DMA
     scratch = [pltpu.VMEM(a.shape, a.dtype) for a in arrays] + [
+        pltpu.VMEM((128, 128), F32), pltpu.VMEM((128, 128), F32), pltpu.VMEM((128, 128), F32),
+        pltpu.VMEM((2, 24), F32),
         pltpu.VMEM((384, 768), BF16), pltpu.VMEM((384, 768), BF16),
         pltpu.VMEM((384, 768), BF16), pltpu.VMEM((384, 768), BF16),
         pltpu.VMEM((3, 128, 128), F32),
@@ -492,22 +504,19 @@
         pltpu.VMEM((8, 4, 2, 24), F32),
         pltpu.VMEM((2, 8, 128), F32), pltpu.VMEM((16, 2, 8, 128), F32),
         pltpu.VMEM((2, 2, 128), F32), pltpu.VMEM((46, 2, 128), F32),
-        dma((count,)), dma((3, 2)), dma((3, 2)), dma((2, 2)), dma((2, 2)), dma((2, 2)), dma((2, 2)),
+        dma((4,)), dma((count,)), dma((3, 2)), dma((3, 2)), dma((2, 2)), dma((2, 2)), dma((2, 2)), dma((2, 2)),
         dma((31,)), dma((31,)), dma((15,)), dma((15,)), dma((46,)), dma((46,)),
     ]
     new_logits, loss = pl.pallas_call(
         functools.partial(kernel, names),
-        out_shape=(
-            jax.ShapeDtypeStruct((128, 128), F32),
-            jax.ShapeDtypeStruct((1, 1), F32),
-        ),
-        in_specs=[vmem] * 4 + [pl.BlockSpec(memory_space=pl.ANY)] * count,
-        out_specs=(vmem, pl.BlockSpec(memory_space=pltpu.SMEM)),
+        out_shape=(pltpu.VMEM((128, 128), F32), pltpu.VMEM((1, 128), F32)),
+        in_specs=[pl.BlockSpec(memory_space=pl.ANY)] * (4 + count),
+        out_specs=(vmem, vmem),
         scratch_shapes=scratch,
         compiler_params=pltpu.CompilerParams(collective_id=0, has_side_effects=True),
         name="litho",
     )(mask_logits, target, weight, kernels, *[jnp.asarray(a) for a in arrays])
-    return new_logits, loss.reshape(())
+    return new_logits, loss[0, 0]
 
 
 def solution(mesh):

time: 50.6 us -> 47.8 us (0.945)
  Pallas kernels: 46.5 us -> 45.2 us
  local copies, waits for them, and re-layouts: 1.47 us -> 0.63 us
  between operations: 2.39 us -> 1.8 us
    pallas_call x1, Pallas kernels: 46.5 us -> 45.2 us  [shards(): pl.pallas_call(functools.partial(kernel, names), out_shape=(pltpu.VMEM((1...]
    unnamed x1, local copies, waits for them, and re-layouts: 1.47 us -> 0.63 us
where the time goes in v4:
time: 47.8 us; the launch traced here: 47.7 us
  Pallas kernels  45.2 us (95%)
  between operations  1.8 us (4%)
  local copies, waits for them, and re-layouts  0.63 us (1%)
    pallas_call x1, Pallas kernels, shards(): pl.pallas_call(functools.partial(kernel, names), out_shape=(pltpu.VMEM((1...  45.2 us

profile of v4, /device:TPU:1, one launch (start us, length us, event | category | flops | bytes accessed | tf_op | source)
XLA Modules:
  0.0 47.7 jit_solution(18411020157230118164)
XLA Ops:
  0.6 45.2 %litho.1 = (f32[128,128]{1,0:T(8,128)S(1)}, f32[1,128]{1,0:T(1,128)S(1)}) custom-call(f32[128,128]{1,0:T(8,128)} %args_0_.4, f32[128,128]{1,0:T(8,128)} %args_1_.4, f32[128,128]{1,0:T(8,128)} %args_2_.4, f32[2,24]{1,0:T(2,128)} %args_3_.4, bf16[256,256]{1,0:T(8,128)(2,1)} %constant.50.clone.args_4_, bf16[256,256]{1,0:T(8,128)(2,1)} %constant.51.clone.args_5_, ...), custom_call_target="tpu_custom_call" | custom-call | tf_op jit(solution)/shard_map/litho/pallas_call | solution.py:510
  45.9 0.6 %copy.33 = f32[128,128]{1,0:T(8,128)} copy(f32[128,128]{1,0:T(8,128)S(1)} %get-tuple-element.6) | data formatting | bytes 131072

commit v5 on v4

--- a/solution.py
+++ b/solution.py
@@ -117,7 +117,12 @@
 
 
 def mm(first, second):
-    return dot(first[0], second[0]) + (dot(first[1], second[0]) + dot(first[0], second[1]))
+    if first[0].shape[1] % 128:
+        return dot(first[0], second[0]) + (dot(first[1], second[0]) + dot(first[0], second[1]))
+    return dot(
+        jnp.concatenate([first[0], first[1], first[0]], axis=1),
+        jnp.concatenate([second[0], second[0], second[1]], axis=0),
+    )
 
 
 def build_left(k, left, own):
@@ -205,7 +210,7 @@
     (
         logits_ref, target_ref, weight_ref, bank_ref,
         left_hi, left_lo, left_t_hi, left_t_lo, vert, pack, from_left, from_right,
-        x_buf, y_send, h_buf, r_send, r_buf,
+        x_buf, x_all, y_send, h_buf, r_send, r_buf,
         i_sem, c_sem, vs_sem, vr_sem, hs_sem, hr_sem, es_sem, er_sem,
         xs_sem, xr_sem, ys_sem, yr_sem, rs_sem, rr_sem,
     ) = args[6 + 2 * count :]
@@ -222,8 +227,15 @@
     def at(z_, y_, core_, x_):
         return ((z_ // 4 * 8 + y_) * 2 + core_, z_ % 4 * 4 + x_)
 
-    xz_peers = [at((z + d) % 8, y, core, (x + e) % 4) for d in range(8) for e in range(4) if d + e]
-    yc_peers = [at(z, (y + d) % 8, (core + e) % 2, x) for d in range(8) for e in range(2) if d + e]
+    def hops(d, n):
+        return min(d, n - d)
+
+    xz_steps = [(d, e) for d in range(8) for e in range(4) if d + e]
+    xz_steps.sort(key=lambda s: (-hops(s[0], 8) - hops(s[1], 4), s))
+    xz_peers = [at((z + d) % 8, y, core, (x + e) % 4) for d, e in xz_steps]
+    yc_steps = [(d, e) for d in range(8) for e in range(2) if d + e]
+    yc_steps.sort(key=lambda s: (-hops(s[0], 8), s))
+    yc_peers = [at(z, (y + d) % 8, (core + e) % 2, x) for d, e in yc_steps]
     sides = [
         (row > 0, (row - 1, col)),
         (row < 31, (row + 1, col)),
@@ -306,9 +318,11 @@
             device_id=peer, device_id_type=MESH,
         )
 
+    def drain(ref, sem):
+        pltpu.make_async_copy(ref, ref, sem).wait()
+
     x_copies = [
-        remote(bank_ref, x_buf.at[z, x], xs_sem.at[i], xr_sem.at[i], peer)
-        for i, peer in enumerate(xz_peers)
+        remote(bank_ref, x_buf.at[z, x], xs_sem, xr_sem, peer) for peer in xz_peers
     ]
     for copy in x_copies:
         copy.start()
@@ -383,8 +397,7 @@
             left_t_hi[:, where : where + 128] = high
             left_t_lo[:, where : where + 128] = low
 
-    for copy in x_copies:
-        copy.wait_recv()
+    drain(x_all, xr_sem)
     for c in range(2):
         parts = [
             jnp.concatenate([x_buf[i, p, c : c + 1, :] for i in range(8)], axis=0)
@@ -393,12 +406,12 @@
         y_send[c] = jnp.concatenate(parts + [jnp.zeros((8, 32), F32)], axis=1)
     mine = core * 8 + y
     y_copies = [
-        remote(y_send, h_buf.at[mine], ys_sem.at[i], yr_sem.at[i], peer)
-        for i, peer in enumerate(yc_peers)
+        remote(y_send, h_buf.at[mine], ys_sem, yr_sem, peer) for peer in yc_peers
     ]
     for copy in y_copies:
         copy.start()
     h_buf[mine] = y_send[...]
+    drain(x_all, xs_sem)
 
     arrive(v_copies[0])
     pack_logits(vert[0], 64)
@@ -423,8 +436,7 @@
     )
     spec = spectrum(jax.nn.sigmoid(wide), con)
 
-    for copy in y_copies:
-        copy.wait_recv()
+    drain(h_buf.at[pl.ds(0, 15)], yr_sem)
     bank = spread_bank([h_buf[:, c].reshape(128, 128) for c in range(2)])
     fields = fields_of(spec, bank, con, (left_hi[...], left_lo[...]))
     intensity = intensity_of(fields, con)
@@ -461,21 +473,23 @@
         axis=0,
     )
     slot = 0
-    r_copies = []
-    for stage, peers in enumerate((xz_peers, yc_peers)):
+    stages = (xz_peers, yc_peers)
+    blocks = [r_buf.at[pl.ds(0, 31)], r_buf.at[pl.ds(31, 15)]]
+    for stage, peers in enumerate(stages):
         r_send[stage] = total
-        copies = [
-            remote(r_send.at[stage], r_buf.at[slot + i], rs_sem.at[slot + i], rr_sem.at[slot + i], peer)
-            for i, peer in enumerate(peers)
-        ]
-        for copy in copies:
-            copy.start()
-        for copy in copies:
-            copy.wait_recv()
-        for i in range(len(peers)):
-            total = total + r_buf[slot + i]
+        for i, peer in enumerate(peers):
+            remote(
+                r_send.at[stage], r_buf.at[slot + i], rs_sem.at[stage], rr_sem.at[stage], peer
+            ).start()
+        if stage == 0:
+            for group in v_copies + h_copies + e_copies:
+                sent(group)
+            drain(h_buf.at[pl.ds(0, 15)], ys_sem)
+        else:
+            drain(blocks[0], rs_sem.at[0])
+        drain(blocks[stage], rr_sem.at[stage])
+        total = total + jnp.sum(r_buf[slot : slot + len(peers)], axis=0)
         slot += len(peers)
-        r_copies += copies
 
     squares = jnp.sum(total[0:1, :], axis=1, keepdims=True)
     loss = jnp.sum(total[1:2, :], axis=1, keepdims=True) / CELLS
@@ -483,10 +497,7 @@
     norm = jnp.sqrt(squares / CELLS + EPSILON)
     out_ref[...] = logits - 0.5 * grad / norm
 
-    for group in v_copies + h_copies + e_copies:
-        sent(group)
-    for copy in x_copies + y_copies + r_copies:
-        copy.wait_send()
+    drain(blocks[1], rs_sem.at[1])
 
 
 def shards(mask_logits, target, weight, kernels):
@@ -501,11 +512,11 @@
         pltpu.VMEM((384, 768), BF16), pltpu.VMEM((384, 768), BF16),
         pltpu.VMEM((3, 128, 128), F32),
         pltpu.VMEM((2, 384, 128), F32), pltpu.VMEM((384, 128), F32), pltpu.VMEM((384, 128), F32),
-        pltpu.VMEM((8, 4, 2, 24), F32),
+        pltpu.VMEM((8, 4, 2, 24), F32), pltpu.VMEM((31, 2, 24), F32),
         pltpu.VMEM((2, 8, 128), F32), pltpu.VMEM((16, 2, 8, 128), F32),
         pltpu.VMEM((2, 2, 128), F32), pltpu.VMEM((46, 2, 128), F32),
         dma((4,)), dma((count,)), dma((3, 2)), dma((3, 2)), dma((2, 2)), dma((2, 2)), dma((2, 2)), dma((2, 2)),
-        dma((31,)), dma((31,)), dma((15,)), dma((15,)), dma((46,)), dma((46,)),
+        dma(()), dma(()), dma(()), dma(()), dma((2,)), dma((2,)),
     ]
     new_logits, loss = pl.pallas_call(
         functools.partial(kernel, names),

time: 47.8 us -> 45.4 us (0.950)
  Pallas kernels: 45.2 us -> 42.8 us
    pallas_call x1, Pallas kernels: 45.2 us -> 42.8 us  [shards(): pl.pallas_call(functools.partial(kernel, names), out_shape=(pltpu.VMEM((1...]
where the time goes in v5:
time: 45.4 us; the launch traced here: 45.2 us
  Pallas kernels  42.8 us (94%)
  between operations  1.8 us (4%)
  local copies, waits for them, and re-layouts  0.63 us (1%)
    pallas_call x1, Pallas kernels, shards(): pl.pallas_call(functools.partial(kernel, names), out_shape=(pltpu.VMEM((1...  42.8 us

profile of v5, /device:TPU:1, one launch (start us, length us, event | category | flops | bytes accessed | tf_op | source)
XLA Modules:
  0.0 45.2 jit_solution(10651008777754113641)
XLA Ops:
  0.6 42.8 %litho.1 = (f32[128,128]{1,0:T(8,128)S(1)}, f32[1,128]{1,0:T(1,128)S(1)}) custom-call(f32[128,128]{1,0:T(8,128)} %args_0_.4, f32[128,128]{1,0:T(8,128)} %args_1_.4, f32[128,128]{1,0:T(8,128)} %args_2_.4, f32[2,24]{1,0:T(2,128)} %args_3_.4, bf16[256,256]{1,0:T(8,128)(2,1)} %constant.50.clone.args_4_, bf16[256,256]{1,0:T(8,128)(2,1)} %constant.51.clone.args_5_, ...), custom_call_target="tpu_custom_call" | custom-call | tf_op jit(solution)/shard_map/litho/pallas_call | solution.py:521
  43.4 0.6 %copy.33 = f32[128,128]{1,0:T(8,128)} copy(f32[128,128]{1,0:T(8,128)S(1)} %get-tuple-element.6) | data formatting | bytes 131072
